TPU v7x, 256 devices: a whole 4x4x8 slice. The times are simulated.
256 devices in a mesh: dp: 16 (over z, core), tensor: 16 (over x, y).
Axes of the slice: x: 4, y: 4, z: 8, core: 2. Of those that a mesh axis runs over, the one named last changes fastest.
Arguments:
- inputs: bfloat16 [4096, 6144], P('dp'), may hold values from -6 to 6
- grad_hidden: bfloat16 [4096, 24576], P('dp', 'tensor'), may hold values from -6 to 6
- w_blocks: bfloat16 [16, 288, 128, 128], P('tensor', 'dp'), may hold values from -0.15625 to 0.15625
- block_ids: int32 [16, 288], P('tensor', 'dp'), may hold values from 0 to 575, as said below
- counts: int32 [16, 16], P('tensor', 'dp'), may hold values from 1 to 18, 144 in all within a row
Outputs:
- hidden: bfloat16 [4096, 24576], P('dp', 'tensor')
- grad_inputs: bfloat16 [4096, 6144], P('dp', 'tensor')
- grad_blocks: bfloat16 [16, 288, 128, 128], P('tensor', 'dp')
Inputs may be any that keep to these rules, and one draw needn't show every extreme that they name: `block_ids`: within one tensor index all 288 ids are distinct. Each row of counts sums to 144.
All inputs are finite; a program needn't handle non-finite values. No bound on the sum of `counts` on one device may be relied on, other than what follows from the above.
Results may differ from a plain program's by a relative error of at most 0.023.
Values may be sent and summed in bfloat16 or wider, within the bound.
A program may use at most 128 MiB of HBM per device.

v0:
```python
import math

import jax
import jax.numpy as jnp
from jax import lax
from jax.sharding import PartitionSpec as P

GELU_C = 0.7978845608028654
GELU_A = 0.044715


def gelu_value(values):
    inner_arg = GELU_C * (values + GELU_A * values * values * values)
    return 0.5 * values * (1.0 + jnp.tanh(inner_arg))


def gelu_slope(values):
    inner_arg = GELU_C * (values + GELU_A * values * values * values)
    tanh_value = jnp.tanh(inner_arg)
    return 0.5 * (1.0 + tanh_value) + 0.5 * values * (1.0 - tanh_value * tanh_value) * GELU_C * (
        1.0 + 3.0 * GELU_A * values * values
    )


def select_live(gathered, capacity, col_blocks):
    blocks = gathered[0][0]
    ids_row = gathered[1][0]
    owner_counts = gathered[2][0]
    slot_total = ids_row.shape[0]
    live_total = slot_total // 2
    slot_index = jnp.arange(slot_total, dtype=jnp.int32)
    is_live = slot_index % capacity < owner_counts[slot_index // capacity]
    live_order = jnp.argsort(jnp.where(is_live, 0, 1).astype(jnp.int32), stable=True)[:live_total]
    live_ids = ids_row[live_order]
    block_size = blocks.shape[-1]
    grouped = (
        blocks[live_order].reshape(live_total // 16, 16, block_size, block_size),
        (live_ids // col_blocks).reshape(live_total // 16, 16),
        (live_ids % col_blocks).reshape(live_total // 16, 16),
    )
    return (grouped, live_order)


def one_hot(indices, length, dtype):
    return (indices[:, None] == jnp.arange(length, dtype=jnp.int32)[None, :]).astype(dtype)


def per_device(inputs, grad_hidden, w_blocks, block_ids, counts):
    tok_rows, model_width = inputs.shape
    block_size = w_blocks.shape[-1]
    row_blocks = model_width // block_size
    capacity = w_blocks.shape[1]
    col_blocks = grad_hidden.shape[1] // block_size
    group_count = lax.axis_size("dp")
    x_blocks = inputs.reshape(tok_rows, row_blocks, block_size)
    gathered = (
        lax.all_gather(w_blocks, "dp", axis=1, tiled=True),
        lax.all_gather(block_ids, "dp", axis=1, tiled=True),
        lax.all_gather(counts, "dp", axis=1, tiled=True),
    )
    forward_pieces, forward_order = select_live(gathered, capacity, col_blocks)

    def pick_rows(rows_here):
        rows_hot = one_hot(rows_here, row_blocks, jnp.bfloat16)
        return jnp.einsum(
            "trb,gr->tgb", x_blocks, rows_hot, preferred_element_type=jnp.float32
        ).astype(jnp.bfloat16)

    def forward_group(running, group_data):
        block_piece, rows_here, cols_here = group_data
        x_rows = pick_rows(rows_here)
        product = jnp.einsum(
            "tgb,gbc->tgc", x_rows, block_piece, preferred_element_type=jnp.float32
        )
        cols_hot = one_hot(cols_here, col_blocks, jnp.float32)
        placed = jnp.einsum("tgc,gk->tkc", product, cols_hot, precision=lax.Precision.HIGHEST)
        return (running + placed, None)

    pre_three, unused = lax.scan(
        forward_group, jnp.zeros((tok_rows, col_blocks, block_size), jnp.float32), forward_pieces
    )
    pre_act = pre_three.reshape(tok_rows, col_blocks * block_size)
    hidden = gelu_value(pre_act).astype(jnp.bfloat16)
    grad_pre = (grad_hidden.astype(jnp.float32) * gelu_slope(pre_act)).astype(jnp.bfloat16)
    grad_three = grad_pre.reshape(tok_rows, col_blocks, block_size)
    backward_pieces, backward_order = (forward_pieces, forward_order)

    def backward_group(running, group_data):
        block_piece, rows_here, cols_here = group_data
        cols_pick = one_hot(cols_here, col_blocks, jnp.bfloat16)
        grad_piece = jnp.einsum(
            "tkc,gk->tgc", grad_three, cols_pick, preferred_element_type=jnp.float32
        ).astype(jnp.bfloat16)
        contrib = jnp.einsum(
            "tgc,gbc->tgb", grad_piece, block_piece, preferred_element_type=jnp.float32
        )
        x_rows = pick_rows(rows_here)
        weight_part = jnp.einsum(
            "tgb,tgc->gbc", x_rows, grad_piece, preferred_element_type=jnp.float32
        )
        rows_place = one_hot(rows_here, row_blocks, jnp.float32)
        placed = jnp.einsum("tgb,gr->trb", contrib, rows_place, precision=lax.Precision.HIGHEST)
        return (running + placed, weight_part)

    input_three, weight_parts = lax.scan(
        backward_group, jnp.zeros((tok_rows, row_blocks, block_size), jnp.float32), backward_pieces
    )
    live_total = backward_order.shape[0]
    weight_parts = weight_parts.reshape(live_total, block_size, block_size)
    grad_inputs = lax.psum_scatter(
        input_three.reshape(tok_rows, model_width).astype(jnp.bfloat16),
        "tensor",
        scatter_dimension=1,
        tiled=True,
    )
    position = (
        jnp.full((capacity * group_count,), -1, jnp.int32)
        .at[backward_order]
        .set(jnp.arange(live_total, dtype=jnp.int32))
    )
    grad_scale = 1.0 / math.sqrt(tok_rows * group_count)
    picked = weight_parts[jnp.maximum(position, 0)]
    summed = lax.psum_scatter(
        jnp.where((position >= 0)[:, None, None], picked, 0.0).astype(jnp.bfloat16),
        "dp",
        scatter_dimension=0,
        tiled=True,
    ).astype(jnp.float32)
    grad_blocks = (summed * grad_scale).astype(jnp.bfloat16)[None]
    return (hidden, grad_inputs, grad_blocks)


def solution(mesh):
    in_specs = (
        P("dp", None),
        P("dp", "tensor"),
        P("tensor", "dp", None, None),
        P("tensor", "dp"),
        P("tensor", "dp"),
    )
    out_specs = (P("dp", "tensor"), P("dp", "tensor"), P("tensor", "dp", None, None))
    return jax.shard_map(
        per_device, mesh=mesh, in_specs=in_specs, out_specs=out_specs, check_vma=False
    )
```

profile of v0, /device:TPU:28, one launch (start us, length us, event | category | flops | bytes accessed | tf_op | source)
XLA Modules:
  0.0 544.8 jit_solution(3201787974582969719)
XLA Ops:
  12.0 16.4 %all-reduce.2 = (s32[288]{0:T(512)S(1)}, s32[16]{0:T(128)S(1)}) all-reduce(s32[288]{0:T(512)S(1)} %bitcast_dynamic-update-slice_fusion.1, s32[16]{0:T(128)S(1)} %bitcast_dynamic-update-slice_fusion), channel_id=1, replica_groups=mesh['dp'=16,'tensor'=16] {'dp'}, use_global_device_ids=true, to_apply=%add | all-reduce | flops 304 | bytes 2432 | tf_op jit(solution)/shard_map/squeeze | solution.py:27
  29.5 4.5 fusion.45
  33.9 5.5 %fusion.44 = s32[288]{0:T(512)S(1)} fusion(pred[288]{0:T(512)(128)(4,1)S(1)} %compare_reduce_fusion, pred[288]{0:T(512)(128)(4,1)S(1)} %compare_reduce_fusion.1, pred[288]{0:T(512)(128)(4,1)S(1)} %compare_reduce_fusion.2, pred[288]{0:T(512)(128)(4,1)S(1)} %compare_reduce_fusion.3, pred[288]{0:T(512)(128)(4,1)S(1)} %compare_reduce_fusion.4, ...), kind=kLoop, calls=%fused_computation.93 | loop fusion | flops 4896 | bytes 4932 | tf_op jit(solution)/shard_map/jit(_where)/select_n | solution.py:33
  39.5 3.8 sort.17
  50.2 23.2 %all-gather.2.cloned.1.call-done = bf16[1,288,128,128]{3,2,0,1:T(8,128)(2,1)} async-done(((bf16[1,18,128,128]{3,2,0,1:T(8,128)(2,1)}), bf16[1,288,128,128]{3,2,0,1:T(8,128)(2,1)}) %all-gather.2.cloned.1.call-update) | async-done | bytes 9437200 | tf_op jit(solution)/shard_map/all_gather | solution.py:57
  73.4 11.2 %gather_fusion.1 = bf16[144,128,128]{2,1,0:T(8,128)(2,1)} fusion(bf16[288,128,128]{2,1,0:T(8,128)(2,1)} %bitcast.149, s32[1024]{0:T(1024)S(1)} %pad_clamp_fusion.1), kind=kCustom, calls=%fused_computation.1 | custom fusion | bytes 9437760 | tf_op jit(solution)/shard_map/gather | solution.py:37
  84.6 101.3 %while.24 = (s32[]{:T(128)}, f32[256,12,128]{2,1,0:T(8,128)}, s32[9,16]{1,0:T(8,128)S(1)}, bf16[9,16,128,128]{3,2,1,0:T(8,128)(2,1)}, s32[9,16]{1,0:T(8,128)S(1)...) while((s32[]{:T(128)}, f32[256,12,128]{2,1,0:T(8,128)}, s32[9,16]{1,0:T(8,128)S(1)}, ...), condition=%wide.region_2.3_spmd.clone, body=%wide.region_1.2_spmd.clone.sunk | while | flops 261358528 | bytes 17302000 | solution.py:79
  85.3 2.8 convolution_bitcast_fusion.5
  88.1 3.1 copy.46
  91.2 4.1 bitcast_add_fusion.4
  95.9 2.8 convolution_bitcast_fusion.5
  98.8 3.1 copy.46
  101.9 4.8 bitcast_add_fusion.4
  107.3 2.8 convolution_bitcast_fusion.5
  110.1 3.1 copy.46
  113.2 4.8 bitcast_add_fusion.4
  118.6 2.8 convolution_bitcast_fusion.5
  121.4 3.1 copy.46
  124.5 4.8 bitcast_add_fusion.4
  129.9 2.8 convolution_bitcast_fusion.5
  132.7 3.1 copy.46
  135.8 4.8 bitcast_add_fusion.4
  141.2 2.8 convolution_bitcast_fusion.5
  144.0 3.1 copy.46
  147.1 4.8 bitcast_add_fusion.4
  152.5 2.8 convolution_bitcast_fusion.5
  155.4 3.1 copy.46
  158.5 4.8 bitcast_add_fusion.4
  163.9 2.8 convolution_bitcast_fusion.5
  166.7 3.1 copy.46
  169.8 4.8 bitcast_add_fusion.4
  175.2 2.8 convolution_bitcast_fusion.5
  178.0 3.1 copy.46
  181.1 4.8 bitcast_add_fusion.4
  188.6 3.9 fusion.38
  195.1 180.7 %while.25 = (s32[]{:T(128)}, f32[256,48,128]{2,1,0:T(8,128)}, bf16[9,16,128,128]{3,2,1,0:T(8,128)(2,1)}, s32[9,16]{1,0:T(8,128)S(1)}, bf16[9,16,128,128]{3,2,1,0...) while((s32[]{:T(128)}, f32[256,48,128]{2,1,0:T(8,128)}, ...), condition=%wide.region_4.5_spmd.clone, body=%wide.region_3.4_spmd.clone.sunk | while | flops 637535936 | bytes 40108668 | solution.py:105
  197.8 2.8 convolution_bitcast_fusion.6
  200.6 3.1 copy.50
  203.7 7.2 %bitcast_add_fusion.5 = f32[256,48,128]{2,1,0:T(8,128)} fusion(f32[256,48,128]{2,1,0:T(8,128)} %get-tuple-element.344, pred[]{:T(512)S(6)} %compare.100, f32[256,16,128]{2,1,0:T(8,128)} %copy.50, s32[16]{0:T(128)S(1)} %get-tuple-element.308), kind=kOutput, calls=%fused_computation.22.clone.1 | convolution fusion | flops 305136384 | bytes 14680129 | tf_op jit(solution)/shard_map/while/body/eval_jaxpr/tgb,gr->trb/dot_general | solution.py:102
  219.1 3.1 copy.50
  222.2 9.0 %bitcast_add_fusion.5 = f32[256,48,128]{2,1,0:T(8,128)} fusion(f32[256,48,128]{2,1,0:T(8,128)} %get-tuple-element.344, pred[]{:T(512)S(6)} %compare.100, f32[256,16,128]{2,1,0:T(8,128)} %copy.50, s32[16]{0:T(128)S(1)} %get-tuple-element.308), kind=kOutput, calls=%fused_computation.22.clone.1 | convolution fusion | flops 305136384 | bytes 14680129 | tf_op jit(solution)/shard_map/while/body/eval_jaxpr/tgb,gr->trb/dot_general | solution.py:102
  236.6 2.8 convolution_bitcast_fusion.6
  239.3 3.1 copy.50
  242.4 9.0 %bitcast_add_fusion.5 = f32[256,48,128]{2,1,0:T(8,128)} fusion(f32[256,48,128]{2,1,0:T(8,128)} %get-tuple-element.344, pred[]{:T(512)S(6)} %compare.100, f32[256,16,128]{2,1,0:T(8,128)} %copy.50, s32[16]{0:T(128)S(1)} %get-tuple-element.308), kind=kOutput, calls=%fused_computation.22.clone.1 | convolution fusion | flops 305136384 | bytes 14680129 | tf_op jit(solution)/shard_map/while/body/eval_jaxpr/tgb,gr->trb/dot_general | solution.py:102
  259.6 3.1 copy.50
  262.7 9.0 %bitcast_add_fusion.5 = f32[256,48,128]{2,1,0:T(8,128)} fusion(f32[256,48,128]{2,1,0:T(8,128)} %get-tuple-element.344, pred[]{:T(512)S(6)} %compare.100, f32[256,16,128]{2,1,0:T(8,128)} %copy.50, s32[16]{0:T(128)S(1)} %get-tuple-element.308), kind=kOutput, calls=%fused_computation.22.clone.1 | convolution fusion | flops 305136384 | bytes 14680129 | tf_op jit(solution)/shard_map/while/body/eval_jaxpr/tgb,gr->trb/dot_general | solution.py:102
  279.9 3.1 copy.50
  283.0 9.0 %bitcast_add_fusion.5 = f32[256,48,128]{2,1,0:T(8,128)} fusion(f32[256,48,128]{2,1,0:T(8,128)} %get-tuple-element.344, pred[]{:T(512)S(6)} %compare.100, f32[256,16,128]{2,1,0:T(8,128)} %copy.50, s32[16]{0:T(128)S(1)} %get-tuple-element.308), kind=kOutput, calls=%fused_computation.22.clone.1 | convolution fusion | flops 305136384 | bytes 14680129 | tf_op jit(solution)/shard_map/while/body/eval_jaxpr/tgb,gr->trb/dot_general | solution.py:102
  297.4 2.8 convolution_bitcast_fusion.6
  300.2 3.1 copy.50
  303.3 9.0 %bitcast_add_fusion.5 = f32[256,48,128]{2,1,0:T(8,128)} fusion(f32[256,48,128]{2,1,0:T(8,128)} %get-tuple-element.344, pred[]{:T(512)S(6)} %compare.100, f32[256,16,128]{2,1,0:T(8,128)} %copy.50, s32[16]{0:T(128)S(1)} %get-tuple-element.308), kind=kOutput, calls=%fused_computation.22.clone.1 | convolution fusion | flops 305136384 | bytes 14680129 | tf_op jit(solution)/shard_map/while/body/eval_jaxpr/tgb,gr->trb/dot_general | solution.py:102
  320.5 3.1 copy.50
  323.6 9.0 %bitcast_add_fusion.5 = f32[256,48,128]{2,1,0:T(8,128)} fusion(f32[256,48,128]{2,1,0:T(8,128)} %get-tuple-element.344, pred[]{:T(512)S(6)} %compare.100, f32[256,16,128]{2,1,0:T(8,128)} %copy.50, s32[16]{0:T(128)S(1)} %get-tuple-element.308), kind=kOutput, calls=%fused_computation.22.clone.1 | convolution fusion | flops 305136384 | bytes 14680129 | tf_op jit(solution)/shard_map/while/body/eval_jaxpr/tgb,gr->trb/dot_general | solution.py:102
  338.0 2.8 convolution_bitcast_fusion.6
  340.8 3.1 copy.50
  343.9 9.0 %bitcast_add_fusion.5 = f32[256,48,128]{2,1,0:T(8,128)} fusion(f32[256,48,128]{2,1,0:T(8,128)} %get-tuple-element.344, pred[]{:T(512)S(6)} %compare.100, f32[256,16,128]{2,1,0:T(8,128)} %copy.50, s32[16]{0:T(128)S(1)} %get-tuple-element.308), kind=kOutput, calls=%fused_computation.22.clone.1 | convolution fusion | flops 305136384 | bytes 14680129 | tf_op jit(solution)/shard_map/while/body/eval_jaxpr/tgb,gr->trb/dot_general | solution.py:102
  361.1 3.1 copy.50
  364.1 9.0 %bitcast_add_fusion.5 = f32[256,48,128]{2,1,0:T(8,128)} fusion(f32[256,48,128]{2,1,0:T(8,128)} %get-tuple-element.344, pred[]{:T(512)S(6)} %compare.100, f32[256,16,128]{2,1,0:T(8,128)} %copy.50, s32[16]{0:T(128)S(1)} %get-tuple-element.308), kind=kOutput, calls=%fused_computation.22.clone.1 | convolution fusion | flops 305136384 | bytes 14680129 | tf_op jit(solution)/shard_map/while/body/eval_jaxpr/tgb,gr->trb/dot_general | solution.py:102
  375.8 3.2 convert_element_type.50
  379.0 3.4 copy.28
  383.5 12.5 %gather_fusion.2 = bf16[288,128,128]{2,1,0:T(8,128)(2,1)} fusion(bf16[144,128,128]{2,1,0:T(8,128)(2,1)} %bitcast.145, s32[1024]{0:T(1024)S(1)} %pad_clamp_fusion), kind=kCustom, calls=%fused_computation.2 | custom fusion | bytes 18875520 | tf_op jit(solution)/shard_map/gather | solution.py:122
  396.1 9.3 %select_convert_fusion = bf16[288,128,128]{2,1,0:T(8,128)(2,1)} fusion(bf16[288,128,128]{2,1,0:T(8,128)(2,1)} %gather_fusion.2, pred[288]{0:T(512)(128)(4,1)S(1)} %broadcast_compare_fusion.1), kind=kLoop, calls=%fused_computation.47 | loop fusion | flops 4718592 | bytes 18874656 | tf_op jit(solution)/shard_map/convert_element_type | solution.py:124
  407.6 52.3 %reduce-scatter.7.cloned.1.call-done = bf16[384,256]{1,0:T(8,128)(2,1)} async-done(((bf16[6144,256]{1,0:T(8,128)(2,1)}), bf16[384,256]{1,0:T(8,128)(2,1)}) %reduce-scatter.7.cloned.1.call-update) | async-done | bytes 196624
  461.7 74.6 %reduce-scatter.5.cloned.1.call-done = bf16[18,128,128]{2,1,0:T(8,128)(2,1)} async-done(((bf16[288,128,128]{2,1,0:T(8,128)(2,1)}), bf16[18,128,128]{2,1,0:T(8,128)(2,1)}) %reduce-scatter.5.cloned.1.call-update) | async-done | bytes 589840 | tf_op jit(solution)/shard_map/reduce_scatter | solution.py:123
  (143 shorter events, 91.4 us)
Async XLA Ops:
  7.2 66.2 %all-gather.2.cloned.1.call-start = ((), (), s32[]{:S(2)}) async-start(), calls=%async_computation.2 | async-start | bytes 10027008 | tf_op jit(solution)/shard_map/all_gather | solution.py:57
  7.9 452.1 %reduce-scatter.7.cloned.1.call-start = ((), (), s32[]{:S(2)}) async-start(), calls=%async_computation.4 | async-start | bytes 3342336
  196.8 1.0 copy-start
  210.9 1.2 copy-start.1
  215.3 1.0 copy-start
  231.2 1.2 copy-start.1
  235.5 1.0 copy-start
  251.5 1.2 copy-start.1
  255.8 1.0 copy-start
  271.7 1.2 copy-start.1
  276.1 1.0 copy-start
  292.0 1.2 copy-start.1
  296.4 1.0 copy-start
  312.3 1.2 copy-start.1
  316.7 1.0 copy-start
  332.6 1.2 copy-start.1
  337.0 1.0 copy-start
  352.9 1.2 copy-start.1
  357.2 1.0 copy-start
  373.2 1.2 copy-start.1
  382.4 153.9 %reduce-scatter.5.cloned.1.call-start = ((), (), s32[]{:S(2)}) async-start(), calls=%async_computation.3 | async-start | bytes 10027008 | tf_op jit(solution)/shard_map/reduce_scatter | solution.py:123
  405.4 1.1 copy-start.2
Sparse Core Ops, SparseCore 0:
  9.8 63.5 all-gather.1
  382.5 77.4 reduce-scatter.6
  462.5 73.7 reduce-scatter.4
where the time goes:
time: 548 us; the launch traced here: 545 us
  matrix products  211 us (39%)
  waiting for transfers between devices  151 us (28%)
  local copies, waits for them, and re-layouts  118 us (22%)
  other arithmetic  32.6 us (6%)
  blocking collectives  16.4 us (3%)
  between operations  15.2 us (3%)
    dot_general x9, matrix products, backward_group(): jnp.einsum('tgb,gr->trb', contrib, rows_place, precision=lax.Precision.HI...  79.4 us
    reduce_scatter x1, waiting for transfers between devices, per_device(): lax.psum_scatter(jnp.where((position >= 0)[:, None, None], picked, 0.0).a...  74.6 us
    unnamed x4, waiting for transfers between devices  53 us
    dot_general x9, matrix products, forward_group(): jnp.einsum('tgc,gk->tkc', product, cols_hot, precision=lax.Precision.HIGH...  42.3 us
    transpose x9, local copies, waits for them, and re-layouts, backward_group(): jnp.einsum('tgc,gbc->tgb', grad_piece, block_piece, preferred_element_typ...  27.9 us
    transpose x9, local copies, waits for them, and re-layouts, forward_group(): jnp.einsum('tgb,gbc->tgc', x_rows, block_piece, preferred_element_type=jn...  27.9 us
    dot_general x9, matrix products, forward_group(): jnp.einsum('tgb,gbc->tgc', x_rows, block_piece, preferred_element_type=jn...  25.5 us
    dot_general x9, matrix products, backward_group(): jnp.einsum('tgc,gbc->tgb', grad_piece, block_piece, preferred_element_typ...  25.1 us
  transfers between devices with their start and end apart: 3, of which 3 were waited for; matrix products, arithmetic and copies ran while one was open for 9% of the time, Pallas kernels for 0%

commit v1 on v0

v1 whole, which is shorter than its diff:
```python
import functools
import math

import jax
import jax.numpy as jnp
from jax import lax
from jax.experimental import pallas as pl
from jax.experimental.pallas import tpu as pltpu
from jax.sharding import PartitionSpec as P

GELU_C = 0.7978845608028654
GELU_A = 0.044715


def gelu_value(values):
    inner_arg = GELU_C * (values + GELU_A * values * values * values)
    return 0.5 * values * (1.0 + jnp.tanh(inner_arg))


def gelu_slope(values):
    inner_arg = GELU_C * (values + GELU_A * values * values * values)
    tanh_value = jnp.tanh(inner_arg)
    return 0.5 * (1.0 + tanh_value) + 0.5 * values * (1.0 - tanh_value * tanh_value) * GELU_C * (
        1.0 + 3.0 * GELU_A * values * values
    )


def block_kernel(capacity, col_blocks, ids_ref, counts_ref, x_ref, gh_ref, w_ref,
                 hidden_ref, partial_ref, gg_ref, pre_ref, gp_ref, acc_ref):
    slots = w_ref.shape[0]
    blk = w_ref.shape[-1]

    def slot_info(s):
        live = (s % capacity) < counts_ref[s // capacity]
        bid = ids_ref[s]
        row = pl.multiple_of((bid // col_blocks) * blk, blk)
        col = pl.multiple_of((bid % col_blocks) * blk, blk)
        return live, row, col

    pre_ref[...] = jnp.zeros_like(pre_ref)

    def fwd(s, carry):
        live, row, col = slot_info(s)

        @pl.when(live)
        def _():
            xr = x_ref[:, pl.ds(row, blk)]
            prod = jnp.dot(xr, w_ref[s], preferred_element_type=jnp.float32)
            pre_ref[:, pl.ds(col, blk)] += prod

        return carry

    lax.fori_loop(0, slots, fwd, 0)

    pre = pre_ref[...]
    hidden_ref[...] = gelu_value(pre).astype(hidden_ref.dtype)
    gp_ref[...] = (gh_ref[...].astype(jnp.float32) * gelu_slope(pre)).astype(gp_ref.dtype)
    acc_ref[...] = jnp.zeros_like(acc_ref)

    def bwd(s, carry):
        live, row, col = slot_info(s)

        @pl.when(live)
        def _():
            g = gp_ref[:, pl.ds(col, blk)]
            w = w_ref[s]
            contrib = lax.dot_general(g, w, (((1,), (1,)), ((), ())),
                                      preferred_element_type=jnp.float32)
            acc_ref[:, pl.ds(row, blk)] += contrib
            xr = x_ref[:, pl.ds(row, blk)]
            part = lax.dot_general(xr, g, (((0,), (0,)), ((), ())),
                                   preferred_element_type=jnp.float32)
            gg_ref[s] = part.astype(gg_ref.dtype)

        @pl.when(jnp.logical_not(live))
        def _():
            gg_ref[s] = jnp.zeros((blk, blk), gg_ref.dtype)

        return carry

    lax.fori_loop(0, slots, bwd, 0)
    partial_ref[...] = acc_ref[...].astype(partial_ref.dtype)


def local_pass(x, gh, w, ids, counts, capacity, col_blocks):
    tok, width = x.shape
    ff = gh.shape[1]
    slots, blk, _ = w.shape
    smem = pl.BlockSpec(memory_space=pltpu.SMEM)
    vmem = pl.BlockSpec(memory_space=pltpu.VMEM)
    flops = 3 * 2 * tok * blk * blk * (slots // 2)
    bytes_accessed = 2 * (x.size + gh.size + 2 * w.size + tok * ff + tok * width)
    return pl.pallas_call(
        functools.partial(block_kernel, capacity, col_blocks),
        out_shape=(
            jax.ShapeDtypeStruct((tok, ff), jnp.bfloat16),
            jax.ShapeDtypeStruct((tok, width), jnp.bfloat16),
            jax.ShapeDtypeStruct((slots, blk, blk), jnp.bfloat16),
        ),
        in_specs=[smem, smem, vmem, vmem, vmem],
        out_specs=(vmem, vmem, vmem),
        scratch_shapes=[
            pltpu.VMEM((tok, ff), jnp.float32),
            pltpu.VMEM((tok, ff), jnp.bfloat16),
            pltpu.VMEM((tok, width), jnp.float32),
        ],
        compiler_params=pltpu.CompilerParams(vmem_limit_bytes=60 * 1024 * 1024),
        cost_estimate=pl.CostEstimate(flops=flops, transcendentals=tok * ff * 2,
                                      bytes_accessed=bytes_accessed),
    )(ids, counts, x, gh, w)


def per_device(inputs, grad_hidden, w_blocks, block_ids, counts):
    tok_rows, model_width = inputs.shape
    block_size = w_blocks.shape[-1]
    capacity = w_blocks.shape[1]
    col_blocks = grad_hidden.shape[1] // block_size
    group_count = lax.axis_size("dp")
    w_all = lax.all_gather(w_blocks, "dp", axis=1, tiled=True)[0]
    ids_all = lax.all_gather(block_ids, "dp", axis=1, tiled=True)[0]
    counts_all = lax.all_gather(counts, "dp", axis=1, tiled=True)[0]
    hidden, partial, gg = local_pass(inputs, grad_hidden, w_all, ids_all, counts_all,
                                     capacity, col_blocks)
    grad_inputs = lax.psum_scatter(partial, "tensor", scatter_dimension=1, tiled=True)
    summed = lax.psum_scatter(gg, "dp", scatter_dimension=0, tiled=True).astype(jnp.float32)
    grad_scale = 1.0 / math.sqrt(tok_rows * group_count)
    grad_blocks = (summed * grad_scale).astype(jnp.bfloat16)[None]
    return (hidden, grad_inputs, grad_blocks)


def solution(mesh):
    in_specs = (
        P("dp", None),
        P("dp", "tensor"),
        P("tensor", "dp", None, None),
        P("tensor", "dp"),
        P("tensor", "dp"),
    )
    out_specs = (P("dp", "tensor"), P("dp", "tensor"), P("tensor", "dp", None, None))
    return jax.shard_map(
        per_device, mesh=mesh, in_specs=in_specs, out_specs=out_specs, check_vma=False
    )
```

time: 548 us -> 318 us (0.58)
  matrix products: 211 us -> 0 us
  local copies, waits for them, and re-layouts: 118 us -> 9.08 us
  Pallas kernels: 0 us -> 76.9 us
  waiting for transfers between devices: 151 us -> 197 us
  other arithmetic: 32.6 us -> 2.02 us
    dot_general x72 -> x0, matrix products: 211 us -> none  [the longest x9 79.4 us: backward_group(): jnp.einsum('tgb,gr->trb', contrib, rows_place, precision=lax.Precision.HI...]
    pallas_call x0 -> x1, Pallas kernels: none -> 76.9 us  [local_pass(): pl.pallas_call(functools.partial(block_kernel, capacity, col_blocks), out...]
    transpose x18 -> x0, local copies, waits for them, and re-layouts: 55.7 us -> none  [the longest x9 27.9 us: backward_group(): jnp.einsum('tgc,gbc->tgb', grad_piece, block_piece, preferred_element_typ...]
    gather x4 -> x0, local copies, waits for them, and re-layouts: 26.1 us -> none  [the longest x1 12.5 us: per_device(): picked = weight_parts[jnp.maximum(position, 0)]]
    unnamed x4, waiting for transfers between devices: 53 us -> 78 us
    all_gather x1, waiting for transfers between devices: 23.2 us -> 44.5 us  [per_device(): w_all = lax.all_gather(w_blocks, 'dp', axis=1, tiled=True)[0]]
    while x37 -> x0, local copies, waits for them, and re-layouts: 17.4 us -> none
    convert_element_type x3 -> x0, other arithmetic: 16.4 us -> none  [the longest x1 9.29 us: per_device(): jnp.where((position >= 0)[:, None, None], picked, 0.0).astype(jnp.bfloat16)]
  transfers between devices with their start and end apart: 3 -> 3, of which waited for: 3 -> 3; matrix products, arithmetic and copies ran while one was open for 9% -> 1% of each run, Pallas kernels for 0% -> 0%
where the time goes in v1:
time: 318 us; the launch traced here: 317 us
  waiting for transfers between devices  197 us (62%)
  Pallas kernels  76.9 us (24%)
  blocking collectives  17 us (5%)
  between operations  15.1 us (5%)
  local copies, waits for them, and re-layouts  9.08 us (3%)
    unnamed x4, waiting for transfers between devices  78 us
    pallas_call x1, Pallas kernels, local_pass(): pl.pallas_call(functools.partial(block_kernel, capacity, col_blocks), out...  76.9 us
    reduce_scatter x1, waiting for transfers between devices, per_device(): lax.psum_scatter(gg, 'dp', scatter_dimension=0, tiled=True)  74.6 us
    all_gather x1, waiting for transfers between devices, per_device(): w_all = lax.all_gather(w_blocks, 'dp', axis=1, tiled=True)[0]  44.5 us
    squeeze x1, blocking collectives, per_device(): ids_all = lax.all_gather(block_ids, 'dp', axis=1, tiled=True)[0]  17 us
    unnamed x7, local copies, waits for them, and re-layouts  9.08 us
  transfers between devices with their start and end apart: 3, of which 3 were waited for; matrix products, arithmetic and copies ran while one was open for 1% of the time, Pallas kernels for 0%

profile of v1, /device:TPU:28, one launch (start us, length us, event | category | flops | bytes accessed | tf_op | source)
XLA Modules:
  0.0 317.3 jit_solution(7298181078820835476)
XLA Ops:
  7.2 0.0 all-gather.2.cloned.1.call-start
  7.2 0.7 all-gather.2.cloned.1.call-update
  7.9 0.0 reduce-scatter.7.cloned.1.call-start
  8.6 1.3 dynamic-slice
  10.5 0.7 bitcast_dynamic-update-slice_fusion
  11.2 0.8 bitcast_dynamic-update-slice_fusion.1
  12.0 17.0 %all-reduce.2 = (s32[288]{0:T(512)}, s32[16]{0:T(128)}) all-reduce(s32[288]{0:T(512)S(1)} %bitcast_dynamic-update-slice_fusion.1, s32[16]{0:T(128)S(1)} %bitcast_dynamic-update-slice_fusion), channel_id=1, replica_groups=mesh['dp'=16,'tensor'=16] {'dp'}, use_global_device_ids=true, to_apply=%add | all-reduce | flops 304 | bytes 2432 | tf_op jit(solution)/shard_map/squeeze | solution.py:120
  28.9 44.5 %all-gather.2.cloned.1.call-done = bf16[1,288,128,128]{3,2,0,1:T(8,128)(2,1)} async-done(((bf16[1,18,128,128]{3,2,0,1:T(8,128)(2,1)}), bf16[1,288,128,128]{3,2,0,1:T(8,128)(2,1)}) %all-gather.2.cloned.1.call-update) | async-done | bytes 9437200 | tf_op jit(solution)/shard_map/all_gather | solution.py:119
  73.4 76.9 %shard_map.76 = (bf16[256,1536]{1,0:T(8,128)(2,1)}, bf16[256,6144]{1,0:T(8,128)(2,1)}, bf16[288,128,128]{2,1,0:T(8,128)(2,1)}) custom-call(s32[288]{0:T(512)} %get-tuple-element.9.ids_ref, s32[16]{0:T(128)} %get-tuple-element.10.counts_ref, bf16[256,6144]{1,0:T(8,128)(2,1)} %x_ref.1, bf16[256,1536]{1,0:T(8,128)(2,1)} %gh_ref.1, bf16[288,128,128]{2,1,0:T(8,128)(2,1)} %bitcast.15), custom_call_target="tpu_custom_call" | custom-call | flops 3623878656 | bytes 26738688 | tf_op jit(solution)/shard_map/pallas_call | solution.py:93
  150.3 4.6 %copy.9 = bf16[256,6144]{0,1:T(8,128)(2,1)} copy(bf16[256,6144]{1,0:T(8,128)(2,1)} %get-tuple-element.7) | data formatting | bytes 6291456
  155.0 0.0 reduce-scatter.7.cloned.1.call-update
  155.0 0.0 reduce-scatter.5.cloned.1.call-start
  155.0 0.7 reduce-scatter.5.cloned.1.call-update
  155.7 76.6 %reduce-scatter.7.cloned.1.call-done = bf16[384,256]{1,0:T(8,128)(2,1)} async-done(((bf16[6144,256]{1,0:T(8,128)(2,1)}), bf16[384,256]{1,0:T(8,128)(2,1)}) %reduce-scatter.7.cloned.1.call-update) | async-done | bytes 196624
  232.4 1.7 copy.10
  234.1 74.6 %reduce-scatter.5.cloned.1.call-done = bf16[18,128,128]{2,1,0:T(8,128)(2,1)} async-done(((bf16[288,128,128]{2,1,0:T(8,128)(2,1)}), bf16[18,128,128]{2,1,0:T(8,128)(2,1)}) %reduce-scatter.5.cloned.1.call-update) | async-done | bytes 589840 | tf_op jit(solution)/shard_map/reduce_scatter | solution.py:125
  308.7 2.0 fusion
  (2 shorter events, 0.0 us)
Async XLA Ops:
  7.2 66.2 %all-gather.2.cloned.1.call-start = ((), (), s32[]{:S(2)}) async-start(), calls=%async_computation.2 | async-start | bytes 10027008 | tf_op jit(solution)/shard_map/all_gather | solution.py:119
  7.9 224.5 %reduce-scatter.7.cloned.1.call-start = ((), (), s32[]{:S(2)}) async-start(), calls=%async_computation.4 | async-start | bytes 3342336
  155.0 153.7 %reduce-scatter.5.cloned.1.call-start = ((), (), s32[]{:S(2)}) async-start(), calls=%async_computation.3 | async-start | bytes 10027008 | tf_op jit(solution)/shard_map/reduce_scatter | solution.py:125
Sparse Core Ops, SparseCore 0:
  9.8 63.5 all-gather.1
  155.1 77.2 reduce-scatter.6
  234.9 73.7 reduce-scatter.4

commit v2 on v1

v2 whole, which is shorter than its diff:
```python
import functools
import math

import jax
import jax.numpy as jnp
from jax import lax
from jax.experimental import pallas as pl
from jax.experimental.pallas import tpu as pltpu
from jax.sharding import PartitionSpec as P

GELU_C = 0.7978845608028654
GELU_A = 0.044715
ID_SPLIT = 32
META_ROWS = 8


def gelu_value(values):
    inner_arg = GELU_C * (values + GELU_A * values * values * values)
    return 0.5 * values * (1.0 + jnp.tanh(inner_arg))


def gelu_slope(values):
    inner_arg = GELU_C * (values + GELU_A * values * values * values)
    tanh_value = jnp.tanh(inner_arg)
    return 0.5 * (1.0 + tanh_value) + 0.5 * values * (1.0 - tanh_value * tanh_value) * GELU_C * (
        1.0 + 3.0 * GELU_A * values * values
    )


def slot_info(capacity, col_blocks, blk, ids_ref, counts_ref, s):
    live = (s % capacity) < counts_ref[s // capacity]
    bid = ids_ref[s]
    row = pl.multiple_of((bid // col_blocks) * blk, blk)
    col = pl.multiple_of((bid % col_blocks) * blk, blk)
    return live, row, col


def forward_kernel(capacity, col_blocks, ids_ref, counts_ref, x_ref, xt_ref, gh_ref, w_ref,
                   hidden_ref, gp_ref, gg_ref, pre_ref):
    owners = w_ref.shape[0]
    blk = w_ref.shape[-1]
    slots = owners * capacity
    info = functools.partial(slot_info, capacity, col_blocks, blk, ids_ref, counts_ref)

    pre_ref[...] = jnp.zeros_like(pre_ref)

    def fwd(s, carry):
        live, row, col = info(s)

        @pl.when(live)
        def _():
            w = w_ref[s // capacity, pl.ds(pl.multiple_of((s % capacity) * blk, blk), blk), :]
            xr = x_ref[:, pl.ds(row, blk)]
            pre_ref[:, pl.ds(col, blk)] += jnp.dot(xr, w, preferred_element_type=jnp.float32)

        return carry

    lax.fori_loop(0, slots, fwd, 0)

    pre = pre_ref[...]
    hidden_ref[...] = gelu_value(pre).astype(hidden_ref.dtype)
    gp_ref[...] = (gh_ref[...].astype(jnp.float32) * gelu_slope(pre)).astype(gp_ref.dtype)

    def grads(s, carry):
        live, row, col = info(s)

        @pl.when(live)
        def _():
            g = gp_ref[:, pl.ds(col, blk)]
            xt = xt_ref[pl.ds(row, blk), :]
            gg_ref[s] = jnp.dot(xt, g, preferred_element_type=jnp.float32).astype(gg_ref.dtype)

        @pl.when(jnp.logical_not(live))
        def _():
            gg_ref[s] = jnp.zeros((blk, blk), gg_ref.dtype)

        return carry

    lax.fori_loop(0, slots, grads, 0)


def backward_kernel(capacity, col_blocks, ids_ref, counts_ref, gp_ref, w_ref, partial_ref, acc_ref):
    owners = w_ref.shape[0]
    blk = w_ref.shape[-1]
    slots = owners * capacity
    info = functools.partial(slot_info, capacity, col_blocks, blk, ids_ref, counts_ref)
    acc_ref[...] = jnp.zeros_like(acc_ref)

    def bwd(s, carry):
        live, row, col = info(s)

        @pl.when(live)
        def _():
            w = w_ref[s // capacity, pl.ds(pl.multiple_of((s % capacity) * blk, blk), blk), :]
            g = gp_ref[:, pl.ds(col, blk)]
            acc_ref[:, pl.ds(row, blk)] += lax.dot_general(
                g, w, (((1,), (1,)), ((), ())), preferred_element_type=jnp.float32)

        return carry

    lax.fori_loop(0, slots, bwd, 0)
    parts, _, piece = partial_ref.shape
    for k in range(parts):
        partial_ref[k] = acc_ref[:, k * piece:(k + 1) * piece].astype(partial_ref.dtype)


def forward_pass(x, xt, gh, w, ids, counts, capacity, col_blocks):
    tok, width = x.shape
    ff = gh.shape[1]
    owners, _, blk = w.shape
    slots = owners * capacity
    smem = pl.BlockSpec(memory_space=pltpu.SMEM)
    vmem = pl.BlockSpec(memory_space=pltpu.VMEM)
    return pl.pallas_call(
        functools.partial(forward_kernel, capacity, col_blocks),
        out_shape=(
            jax.ShapeDtypeStruct((tok, ff), jnp.bfloat16),
            jax.ShapeDtypeStruct((tok, ff), jnp.bfloat16),
            jax.ShapeDtypeStruct((slots, blk, blk), jnp.bfloat16),
        ),
        in_specs=[smem, smem, vmem, vmem, vmem, vmem],
        out_specs=(vmem, vmem, vmem),
        scratch_shapes=[pltpu.VMEM((tok, ff), jnp.float32)],
        compiler_params=pltpu.CompilerParams(vmem_limit_bytes=60 * 1024 * 1024),
        cost_estimate=pl.CostEstimate(
            flops=2 * 2 * tok * blk * blk * (slots // 2), transcendentals=2 * tok * ff,
            bytes_accessed=2 * (2 * x.size + 3 * gh.size + w.size + slots * blk * blk)),
    )(ids, counts, x, xt, gh, w)


def backward_pass(gp, w, ids, counts, capacity, col_blocks, width, parts):
    tok, ff = gp.shape
    owners, _, blk = w.shape
    slots = owners * capacity
    smem = pl.BlockSpec(memory_space=pltpu.SMEM)
    vmem = pl.BlockSpec(memory_space=pltpu.VMEM)
    return pl.pallas_call(
        functools.partial(backward_kernel, capacity, col_blocks),
        out_shape=jax.ShapeDtypeStruct((parts, tok, width // parts), jnp.bfloat16),
        in_specs=[smem, smem, vmem, vmem],
        out_specs=vmem,
        scratch_shapes=[pltpu.VMEM((tok, width), jnp.float32)],
        compiler_params=pltpu.CompilerParams(vmem_limit_bytes=60 * 1024 * 1024),
        cost_estimate=pl.CostEstimate(
            flops=2 * tok * blk * blk * (slots // 2), transcendentals=0,
            bytes_accessed=2 * (gp.size + w.size + tok * width)),
    )(ids, counts, gp, w)


def per_device(inputs, grad_hidden, w_blocks, block_ids, counts):
    tok_rows, model_width = inputs.shape
    block_size = w_blocks.shape[-1]
    capacity = w_blocks.shape[1]
    col_blocks = grad_hidden.shape[1] // block_size
    group_count = lax.axis_size("dp")
    parts = lax.axis_size("tensor")
    ids_row = block_ids[0]
    meta = jnp.zeros((META_ROWS, block_size), jnp.float32)
    meta = meta.at[0, :capacity].set((ids_row // ID_SPLIT).astype(jnp.float32))
    meta = meta.at[1, :capacity].set((ids_row % ID_SPLIT).astype(jnp.float32))
    meta = meta.at[2, 0].set(counts[0, 0].astype(jnp.float32))
    packed = jnp.concatenate(
        [w_blocks.reshape(capacity * block_size, block_size), meta.astype(jnp.bfloat16)], axis=0)
    gathered = lax.all_gather(packed[None], "dp", axis=0, tiled=True)
    meta_all = gathered[:, capacity * block_size:, :].astype(jnp.float32).astype(jnp.int32)
    ids_all = (meta_all[:, 0, :capacity] * ID_SPLIT + meta_all[:, 1, :capacity]).reshape(-1)
    counts_all = meta_all[:, 2, 0]
    hidden, gp, gg = forward_pass(inputs, inputs.T, grad_hidden, gathered, ids_all, counts_all,
                                  capacity, col_blocks)
    summed = lax.psum_scatter(gg, "dp", scatter_dimension=0, tiled=True).astype(jnp.float32)
    partial = backward_pass(gp, gathered, ids_all, counts_all, capacity, col_blocks,
                            model_width, parts)
    grad_inputs = lax.psum_scatter(partial, "tensor", scatter_dimension=0, tiled=True)[0]
    grad_scale = 1.0 / math.sqrt(tok_rows * group_count)
    grad_blocks = (summed * grad_scale).astype(jnp.bfloat16)[None]
    return (hidden, grad_inputs, grad_blocks)


def solution(mesh):
    in_specs = (
        P("dp", None),
        P("dp", "tensor"),
        P("tensor", "dp", None, None),
        P("tensor", "dp"),
        P("tensor", "dp"),
    )
    out_specs = (P("dp", "tensor"), P("dp", "tensor"), P("tensor", "dp", None, None))
    return jax.shard_map(
        per_device, mesh=mesh, in_specs=in_specs, out_specs=out_specs, check_vma=False
    )
```

time: 318 us -> 307 us (0.965)
  Pallas kernels: 76.9 us -> 104 us
  waiting for transfers between devices: 197 us -> 175 us
  blocking collectives: 17 us -> 0 us
  other arithmetic: 2.02 us -> 5.41 us
    reduce_scatter x1, waiting for transfers between devices: 74.6 us -> 35.6 us  [per_device(): lax.psum_scatter(gg, 'dp', scatter_dimension=0, tiled=True)]
    pallas_call x1 -> x2, Pallas kernels: 76.9 us -> 104 us  [the longest x1 67.6 us: forward_pass(): pl.pallas_call(functools.partial(forward_kernel, capacity, col_blocks), o...]
    squeeze x1 -> x0, blocking collectives: 17 us -> none  [per_device(): ids_all = lax.all_gather(block_ids, 'dp', axis=1, tiled=True)[0]]
    all_gather x1, waiting for transfers between devices: 44.5 us -> 59.1 us  [per_device(): gathered = lax.all_gather(packed[None], 'dp', axis=0, tiled=True)]
    unnamed x7 -> x1, local copies, waits for them, and re-layouts: 9.08 us -> 4.68 us
  transfers between devices with their start and end apart: 3 -> 3, of which waited for: 3 -> 3; matrix products, arithmetic and copies ran while one was open for 1% -> 2% of each run, Pallas kernels for 0% -> 12%
where the time goes in v2:
time: 307 us; the launch traced here: 305 us
  waiting for transfers between devices  175 us (57%)
  Pallas kernels  104 us (34%)
  between operations  14.4 us (5%)
  local copies, waits for them, and re-layouts  6.45 us (2%)
  other arithmetic  5.41 us (2%)
    unnamed x4, waiting for transfers between devices  80.5 us
    pallas_call x1, Pallas kernels, forward_pass(): pl.pallas_call(functools.partial(forward_kernel, capacity, col_blocks), o...  67.6 us
    all_gather x1, waiting for transfers between devices, per_device(): gathered = lax.all_gather(packed[None], 'dp', axis=0, tiled=True)  59.1 us
    pallas_call x1, Pallas kernels, backward_pass(): pl.pallas_call(functools.partial(backward_kernel, capacity, col_blocks),...  36.1 us
    reduce_scatter x1, waiting for transfers between devices, per_device(): lax.psum_scatter(gg, 'dp', scatter_dimension=0, tiled=True)  35.6 us
  transfers between devices with their start and end apart: 3, of which 3 were waited for; matrix products, arithmetic and copies ran while one was open for 2% of the time, Pallas kernels for 12%

profile of v2, /device:TPU:28, one launch (start us, length us, event | category | flops | bytes accessed | tf_op | source)
XLA Modules:
  0.0 305.2 jit_solution(11718878765894342606)
XLA Ops:
  7.2 0.0 all-gather.3.cloned.1.call-start
  7.9 0.7 fusion.2
  8.5 0.2 scatter.11
  8.7 1.9 pad_maximum_fusion
  10.7 0.0 all-gather.3.cloned.1.call-update
  10.7 0.0 reduce-scatter.5.cloned.1.call-start
  10.7 4.7 %copy.10 = bf16[256,6144]{0,1:T(8,128)(2,1)} copy(bf16[256,6144]{1,0:T(8,128)(2,1)} %x_ref.1) | data formatting | bytes 6291456 | tf_op args[0]
  15.4 59.1 %all-gather.3.cloned.1.call-done = bf16[36992,128]{1,0:T(8,128)(2,1)} async-done(((bf16[2312,128]{1,0:T(8,128)(2,1)}), bf16[36992,128]{1,0:T(8,128)(2,1)}) %all-gather.3.cloned.1.call-update) | async-done | bytes 9469968 | tf_op jit(solution)/shard_map/all_gather | solution.py:164
  74.5 0.8 convert_convert_fusion
  75.3 0.9 slice_reduce_fusion.counts_ref
  76.2 0.7 add.30.ids_ref
  76.9 67.6 %shard_map.76 = (bf16[256,1536]{1,0:T(8,128)(2,1)}, bf16[256,1536]{1,0:T(8,128)(2,1)}, bf16[288,128,128]{2,1,0:T(8,128)(2,1)}) custom-call(s32[288]{0:T(512)} %add.30.ids_ref, s32[16]{0:T(128)} %slice_reduce_fusion.counts_ref, bf16[256,6144]{1,0:T(8,128)(2,1)} %x_ref.1, bf16[6144,256]{1,0:T(8,128)(2,1)} %bitcast.10, bf16[256,1536]{1,0:T(8,128)(2,1)} %gh_ref.1, ...), custom_call_target="tpu_custom_call" | custom-call | flops 2415919104 | bytes 27557888 | tf_op jit(solution)/shard_map/pallas_call | solution.py:114
  144.5 0.0 reduce-scatter.5.cloned.1.call-update
  144.5 0.0 reduce-scatter.7.cloned.1.call-start
  144.6 36.1 %shard_map.77 = bf16[16,256,384]{2,1,0:T(8,128)(2,1)} custom-call(s32[288]{0:T(512)} %add.30.ids_ref, s32[16]{0:T(128)} %slice_reduce_fusion.counts_ref, bf16[256,1536]{1,0:T(8,128)(2,1)} %get-tuple-element.43.gp_ref, bf16[16,2312,128]{2,1,0:T(8,128)(2,1)} %bitcast.9), custom_call_target="tpu_custom_call" | custom-call | flops 1207959552 | bytes 13402112 | tf_op jit(solution)/shard_map/pallas_call | solution.py:137
  180.7 0.0 reduce-scatter.7.cloned.1.call-update
  180.7 35.6 %reduce-scatter.5.cloned.1.call-done = bf16[18,128,128]{2,1,0:T(8,128)(2,1)} async-done(((bf16[288,128,128]{2,1,0:T(8,128)(2,1)}), bf16[18,128,128]{2,1,0:T(8,128)(2,1)}) %reduce-scatter.5.cloned.1.call-update) | async-done | bytes 589840 | tf_op jit(solution)/shard_map/reduce_scatter | solution.py:170
  216.3 2.0 fusion
  218.3 80.4 %reduce-scatter.7.cloned.1.call-done = bf16[1,256,384]{2,1,0:T(8,128)(2,1)} async-done(((bf16[16,256,384]{2,1,0:T(8,128)(2,1)}), bf16[1,256,384]{2,1,0:T(8,128)(2,1)}) %reduce-scatter.7.cloned.1.call-update) | async-done | bytes 196624
  (3 shorter events, 0.1 us)
Async XLA Ops:
  7.2 67.3 %all-gather.3.cloned.1.call-start = ((), (), s32[]{:S(2)}) async-start(), calls=%async_computation.3 | async-start | bytes 10061824 | tf_op jit(solution)/shard_map/all_gather | solution.py:164
  10.7 205.6 %reduce-scatter.5.cloned.1.call-start = ((), (), s32[]{:S(2)}) async-start(), calls=%async_computation.2 | async-start | bytes 10027008 | tf_op jit(solution)/shard_map/reduce_scatter | solution.py:170
  144.5 154.2 %reduce-scatter.7.cloned.1.call-start = ((), (), s32[]{:S(2)}) async-start(), calls=%async_computation.4 | async-start | bytes 3342336
Sparse Core Ops, SparseCore 0:
  10.8 63.6 all-gather.2
  144.7 71.5 reduce-scatter.4
  220.5 78.1 reduce-scatter.6
